TPU v7x, 512 devices: a whole 4x4x16 slice. The times are simulated.
512 devices in a mesh: var: 32 (over z_lo, y, core), head: 16 (over z_hi, x).
Axes of the slice: x: 4, y: 4, z: 16 (z_hi: 4, z_lo: 4; z = z_hi * 4 + z_lo), core: 2. Of those that a mesh axis runs over, the one named last changes fastest.
Arguments:
- queries: bfloat16 [16384, 8192], P('var', 'head'), may hold values from -5 to 5
- ablated: int32 [16384], P('var'), may hold values from 0 to 63
- head_keep: int32 [32, 64], P(None, 'head'), may hold values 0 or 1
- k_cache: bfloat16 [32, 2048, 1024], P('var', 'head'), may hold values from -4 to 4
- v_cache: bfloat16 [32, 2048, 1024], P('var', 'head'), may hold values from -40 to 40
- lengths: int32 [32], P('var'), may hold values from 512 to 2048, as said below
- out_weight: bfloat16 [8192, 4096], P('head', 'var'), may hold values from -0.125 to 0.125
- residual: bfloat16 [16384, 4096], P('var', 'head'), may hold values from -6 to 6
Outputs:
- patched: bfloat16 [16384, 4096], P('var', 'head')
Inputs may be any that keep to these rules, and one draw needn't show every extreme that they name: `lengths`: one prompt has exactly 2048 live positions.
All inputs are finite; a program needn't handle non-finite values. No bound on the sum of `head_keep` on one device may be relied on, other than what follows from the above.
Results may differ from a plain program's by a relative error of at most 0.012.
Values may be sent and summed in bfloat16 or wider, within the bound.
No kernel may reach another device: no remote copies, remote signals or barrier semaphores. Data moves between devices by JAX's collectives and lax.ppermute only.
A program may use at most 64 MiB of HBM per device.

v0:
```python
import math
import jax
import jax.numpy as jnp
from jax import lax
from jax.sharding import PartitionSpec as P

HEADS = 64
KVH = 8
HD = 128


def attend(query_rows, full_keys, full_values, prompt_length):
    local_heads = query_rows.shape[1]
    group_size = HEADS // KVH
    score_scale = 1.0 / math.sqrt(HD)
    visible = jnp.arange(full_keys.shape[0]) < prompt_length
    pieces_out = []
    for column_pair in range(local_heads // 2):
        kv_index = 2 * column_pair // group_size
        query_pair = query_rows[:, 2 * column_pair : 2 * column_pair + 2, :]
        scores = (
            jnp.einsum(
                "rhd,td->hrt",
                query_pair,
                full_keys[:, kv_index, :],
                preferred_element_type=jnp.float32,
            )
            * score_scale
        )
        scores = jnp.where(visible, scores, -jnp.inf)
        row_max = jnp.max(scores, axis=-1, keepdims=True)
        exponent = jnp.exp(scores - row_max)
        probs = (exponent / jnp.sum(exponent, axis=-1, keepdims=True)).astype(jnp.bfloat16)
        outputs = jnp.einsum(
            "hrt,td->rhd", probs, full_values[:, kv_index, :], preferred_element_type=jnp.float32
        )
        pieces_out.append(outputs.astype(jnp.bfloat16))
    return jnp.concatenate(pieces_out, axis=1)


def project(gated, out_weight):
    partial_value = jnp.dot(
        gated,
        lax.all_gather(out_weight, "var", axis=1, tiled=True),
        preferred_element_type=jnp.float32,
    )
    return lax.psum_scatter(
        partial_value.astype(jnp.bfloat16), "head", scatter_dimension=1, tiled=True
    )


def per_device(queries, ablated, head_keep, k_cache, v_cache, lengths, out_weight, residual):
    row_count, feature_count = queries.shape
    var_count = lax.axis_size("var")
    head_count = lax.axis_size("head")
    local_heads = head_keep.shape[1]
    per_prompt = row_count // var_count
    head_position = lax.axis_index("head")
    copies = max(1, head_count // KVH)
    local_positions = k_cache.shape[1]
    stacked = jnp.stack([k_cache[0], v_cache[0]]).reshape(2, local_positions, KVH, HD)
    stacked = jnp.repeat(stacked, copies, axis=2)
    arrived_kv = lax.all_to_all(stacked, "head", split_axis=2, concat_axis=1, tiled=True)
    full_keys = arrived_kv[0]
    full_values = arrived_kv[1]
    prompt_keep = jnp.repeat(head_keep, per_prompt, axis=0)
    heads_here = head_position * local_heads + jnp.arange(local_heads)
    kept_heads = jnp.where(ablated[:, None] != heads_here[None, :], prompt_keep, 0).astype(
        jnp.bfloat16
    )
    grouped = queries.reshape(var_count, per_prompt, feature_count)
    arrived = lax.all_to_all(grouped, "var", split_axis=0, concat_axis=0, tiled=True)
    head_out = attend(
        arrived.reshape(row_count, local_heads, HD), full_keys, full_values, lengths[0]
    )
    returned = lax.all_to_all(
        head_out.reshape(var_count, per_prompt, feature_count),
        "var",
        split_axis=0,
        concat_axis=0,
        tiled=True,
    )
    gated = (returned.reshape(row_count, local_heads, HD) * kept_heads[:, :, None]).reshape(
        row_count, feature_count
    )
    projected = project(gated, out_weight)
    return (residual.astype(jnp.float32) + projected.astype(jnp.float32)).astype(jnp.bfloat16)


def solution(mesh):
    return jax.shard_map(
        per_device,
        mesh=mesh,
        in_specs=(
            P("var", "head"),
            P("var"),
            P(None, "head"),
            P("var", "head", None),
            P("var", "head", None),
            P("var"),
            P("head", "var"),
            P("var", "head"),
        ),
        out_specs=P("var", "head"),
        check_vma=False,
    )
```

profile of v0, /device:TPU:8, one launch (start us, length us, event | category | flops | bytes accessed | tf_op | source)
XLA Modules:
  0.0 328.7 jit_solution(7150349831020283195)
XLA Ops:
  6.5 9.3 %all-to-all-start.1 = ((bf16[32,16,512]{2,1,0:T(8,128)(2,1)}), bf16[32,16,512]{2,1,0:T(8,128)(2,1)S(1)}, u32[]{:S(2)}, u32[]{:S(2)}) async-start(bf16[32,16,512]{2,1,0:T(8,128)(2,1)} %bitcast.62), calls=%async_computation.1 | async-start | bytes 1048576 | tf_op jit(solution)/shard_map/all_to_all | solution.py:72
  15.9 1.2 copy_bitcast_fusion
  17.0 13.6 %all-to-all-done.1 = bf16[32,16,512]{2,1,0:T(8,128)(2,1)S(1)} async-done(((bf16[32,16,512]{2,1,0:T(8,128)(2,1)}), bf16[32,16,512]{2,1,0:T(8,128)(2,1)S(1)}, u32[]{:S(2)}, u32[]{:S(2)}) %all-to-all-start.1) | async-done | bytes 524320 | tf_op jit(solution)/shard_map/all_to_all | solution.py:72
  30.7 1.2 broadcast_in_dim.27
  31.9 14.6 %all-to-all-start = ((bf16[2,128,16,128]{3,1,0,2:T(8,128)(2,1)}), bf16[2,128,16,128]{3,1,0,2:T(8,128)(2,1)S(1)}, u32[]{:S(2)}, u32[]{:S(2)}) async-start(bf16[2,128,16,128]{3,1,0,2:T(8,128)(2,1)} %bitcast), calls=%async_computation | async-start | bytes 2097152 | tf_op jit(solution)/shard_map/all_to_all | solution.py:63
  46.5 0.0 all-gather.2.cloned.1.call-start
  46.6 0.7 all-gather.2.cloned.1.call-update
  47.9 0.1 reshape.73
  48.0 0.4 fusion.46
  48.4 50.3 %all-to-all-done = bf16[2,128,16,128]{3,1,0,2:T(8,128)(2,1)S(1)} async-done(((bf16[2,128,16,128]{3,1,0,2:T(8,128)(2,1)}), bf16[2,128,16,128]{3,1,0,2:T(8,128)(2,1)S(1)}, u32[]{:S(2)}, u32[]{:S(2)}) %all-to-all-start) | async-done | bytes 1048608 | tf_op jit(solution)/shard_map/all_to_all | solution.py:63
  98.8 0.1 fusion.45
  98.9 6.1 %fusion.52 = (f32[2,512]{1,0:T(2,128)S(1)}, f32[2,512,2048]{1,2,0:T(8,128)}) fusion(pred[2048]{0:T(1024)(128)(4,1)S(1)} %iota_compare_fusion, bf16[2048,128,1]{1,0,2:T(8,128)(2,1)S(1)} %bitcast.66, bf16[512,2,128]{2,1,0:T(2,128)(2,1)S(1)} %get-tuple-element.7), kind=kOutput, calls=%fused_computation.51 | convolution fusion | flops 545261568 | bytes 9181184 | tf_op jit(solution)/shard_map/sub | solution.py:32
  104.9 6.1 %fusion.47 = (f32[2,512]{1,0:T(2,128)S(1)}, f32[2,512,2048]{1,2,0:T(8,128)}) fusion(pred[2048]{0:T(1024)(128)(4,1)S(1)} %iota_compare_fusion, bf16[2048,128,1]{1,0,2:T(8,128)(2,1)S(1)} %bitcast.67, bf16[512,2,128]{2,1,0:T(2,128)(2,1)S(1)} %get-tuple-element.8), kind=kOutput, calls=%fused_computation.50 | convolution fusion | flops 545261568 | bytes 9181184 | tf_op jit(solution)/shard_map/sub | solution.py:32
  111.0 0.0 copy-start.3
  111.0 4.3 %fusion.20 = bf16[512,2,128]{0,2,1:T(8,128)(2,1)S(1)} fusion(bf16[2048,128,1]{1,0,2:T(8,128)(2,1)S(1)} %bitcast.64, f32[2,512,2048]{1,2,0:T(8,128)} %get-tuple-element.12, f32[2,512]{1,0:T(2,128)S(1)} %get-tuple-element.11), kind=kOutput, calls=%fused_computation.25 | convolution fusion | flops 541196288 | bytes 9179136 | tf_op jit(solution)/shard_map/hrt,td->rhd/dot_general | solution.py:34
  115.3 1.5 copy-done.3
  116.8 0.0 copy-start.1
  116.8 0.0 copy-start.2
  116.8 0.8 fusion.21
  117.7 0.3 copy.27
  118.0 1.0 reshape.74
  119.0 11.7 %all-to-all-start.2 = ((bf16[32,16,512]{2,1,0:T(8,128)(2,1)}), bf16[32,16,512]{2,1,0:T(8,128)(2,1)S(1)}, u32[]{:S(2)}, u32[]{:S(2)}) async-start(bf16[32,16,512]{2,1,0:T(8,128)(2,1)} %reshape.74), calls=%async_computation.2 | async-start | bytes 1048576 | tf_op jit(solution)/shard_map/all_to_all | solution.py:76
  130.6 0.2 reduce-scatter.2.cloned.1.call-start
  130.9 0.0 copy-done.1
  130.9 0.1 broadcast_in_dim.30
  131.0 0.1 reshape.76
  131.1 0.0 copy-done.2
  131.1 0.1 select_convert_fusion
  131.2 0.2 copy.28
  131.3 0.0 copy-start
  131.4 15.4 %all-to-all-done.2 = bf16[32,16,512]{2,1,0:T(8,128)(2,1)S(1)} async-done(((bf16[32,16,512]{2,1,0:T(8,128)(2,1)}), bf16[32,16,512]{2,1,0:T(8,128)(2,1)S(1)}, u32[]{:S(2)}, u32[]{:S(2)}) %all-to-all-start.2) | async-done | bytes 524320 | tf_op jit(solution)/shard_map/all_to_all | solution.py:76
  146.7 2.9 all-gather.2.cloned.1.call-done
  149.6 0.6 mul.25
  150.2 6.5 %convolution_convert_fusion = bf16[512,4096]{1,0:T(8,128)(2,1)} fusion(bf16[512,4096]{1,0:T(8,128)(2,1)} %all-gather.2.cloned.1.call-done, bf16[512,512]{1,0:T(8,128)(2,1)S(1)} %bitcast.63, bf16[64,8,4,128]{3,2,1,0:T(4,128)(2,1)S(1)} %bitcast.61), kind=kOutput, calls=%fused_computation.14 | convolution fusion | flops 2149842944 | bytes 9437184 | tf_op jit(solution)/shard_map/dot_general | solution.py:42
  156.7 0.0 reduce-scatter.2.cloned.1.call-update
  156.7 163.5 %reduce-scatter.2.cloned.1.call-done = bf16[512,256]{1,0:T(8,128)(2,1)} async-done(((bf16[512,4096]{1,0:T(8,128)(2,1)}), bf16[512,256]{1,0:T(8,128)(2,1)}) %reduce-scatter.2.cloned.1.call-update) | async-done | bytes 262160 | tf_op jit(solution)/shard_map/reduce_scatter | solution.py:47
  320.1 0.0 copy-done
  320.1 1.7 add_convert_fusion
  (3 shorter events, 0.1 us)
Async XLA Ops:
  6.5 24.1 %all-to-all-start.1 = ((bf16[32,16,512]{2,1,0:T(8,128)(2,1)}), bf16[32,16,512]{2,1,0:T(8,128)(2,1)S(1)}, u32[]{:S(2)}, u32[]{:S(2)}) async-start(bf16[32,16,512]{2,1,0:T(8,128)(2,1)} %bitcast.62), calls=%async_computation.1 | async-start | bytes 1048576 | tf_op jit(solution)/shard_map/all_to_all | solution.py:72
  31.9 66.9 %all-to-all-start = ((bf16[2,128,16,128]{3,1,0,2:T(8,128)(2,1)}), bf16[2,128,16,128]{3,1,0,2:T(8,128)(2,1)S(1)}, u32[]{:S(2)}, u32[]{:S(2)}) async-start(bf16[2,128,16,128]{3,1,0,2:T(8,128)(2,1)} %bitcast), calls=%async_computation | async-start | bytes 2097152 | tf_op jit(solution)/shard_map/all_to_all | solution.py:63
  46.5 103.0 %all-gather.2.cloned.1.call-start = ((), (), s32[]{:S(2)}) async-start(), calls=%async_computation.4 | async-start | bytes 4325376 | tf_op jit(solution)/shard_map/all_gather | solution.py:44
  111.0 5.8 %copy-start.3 = (f32[2,512,2048]{1,2,0:T(8,128)S(1)}, f32[2,512,2048]{1,2,0:T(8,128)}, u32[]{:S(2)}) copy-start(f32[2,512,2048]{1,2,0:T(8,128)} %get-tuple-element.10) | copy-start | bytes 25165828
  116.8 14.1 %copy-start.1 = (s32[32,4]{0,1:T(4,128)S(1)}, s32[32,4]{0,1:T(4,128)}, u32[]{:S(2)}) copy-start(s32[32,4]{0,1:T(4,128)} %param.10) | copy-start | bytes 1540
  116.8 14.3 %copy-start.2 = (s32[512]{0:T(512)S(1)}, s32[512]{0:T(512)}, u32[]{:S(2)}) copy-start(s32[512]{0:T(512)} %param.9) | copy-start | bytes 6148
  119.0 27.8 %all-to-all-start.2 = ((bf16[32,16,512]{2,1,0:T(8,128)(2,1)}), bf16[32,16,512]{2,1,0:T(8,128)(2,1)S(1)}, u32[]{:S(2)}, u32[]{:S(2)}) async-start(bf16[32,16,512]{2,1,0:T(8,128)(2,1)} %reshape.74), calls=%async_computation.2 | async-start | bytes 1048576 | tf_op jit(solution)/shard_map/all_to_all | solution.py:76
  130.6 189.5 %reduce-scatter.2.cloned.1.call-start = ((), (), s32[]{:S(2)}) async-start(), calls=%async_computation.5 | async-start | bytes 4456448 | tf_op jit(solution)/shard_map/reduce_scatter | solution.py:47
  131.3 188.8 %copy-start = (bf16[512,256]{1,0:T(8,128)(2,1)S(1)}, bf16[512,256]{1,0:T(8,128)(2,1)}, u32[]{:S(2)}) copy-start(bf16[512,256]{1,0:T(8,128)(2,1)} %param.15) | copy-start | bytes 786436
Sparse Core Ops, SparseCore 0:
  49.4 100.1 all-gather.1
  156.8 163.2 reduce-scatter.1
where the time goes:
time: 329 us
  waiting for transfers between devices  246 us (75%)
  starting transfers between devices  35.9 us (11%)
  matrix products  23.6 us (7%)
  between operations  14.2 us (4%)
  local copies, waits for them, and re-layouts  5.61 us (2%)
    reduce_scatter x1, waiting for transfers between devices, project(): lax.psum_scatter(partial_value.astype(jnp.bfloat16), 'head', scatter_dime...  163 us
    all_to_all x1, waiting for transfers between devices, per_device(): lax.all_to_all(stacked, 'head', split_axis=2, concat_axis=1, tiled=True)  50.3 us
    all_to_all x1, waiting for transfers between devices, per_device(): lax.all_to_all(head_out.reshape(var_count, per_prompt, feature_count), 'v...  15.4 us
    all_to_all x1, starting transfers between devices, per_device(): lax.all_to_all(stacked, 'head', split_axis=2, concat_axis=1, tiled=True)  14.6 us
    all_to_all x1, waiting for transfers between devices, per_device(): lax.all_to_all(grouped, 'var', split_axis=0, concat_axis=0, tiled=True)  13.6 us
    sub x2, matrix products, attend(): exponent = jnp.exp(scores - row_max)  12.2 us
    all_to_all x1, starting transfers between devices, per_device(): lax.all_to_all(head_out.reshape(var_count, per_prompt, feature_count), 'v...  11.7 us
    all_to_all x1, starting transfers between devices, per_device(): lax.all_to_all(grouped, 'var', split_axis=0, concat_axis=0, tiled=True)  9.34 us
  transfers between devices with their start and end apart: 5, of which 5 were waited for; matrix products, arithmetic and copies ran while one was open for 6% of the time, Pallas kernels for 0%

commit v1 on v0

--- a/solution.py
+++ b/solution.py
@@ -60,7 +60,10 @@
     local_positions = k_cache.shape[1]
     stacked = jnp.stack([k_cache[0], v_cache[0]]).reshape(2, local_positions, KVH, HD)
     stacked = jnp.repeat(stacked, copies, axis=2)
-    arrived_kv = lax.all_to_all(stacked, "head", split_axis=2, concat_axis=1, tiled=True)
+    arrived_kv = jnp.concatenate(
+        lax.all_to_all(jnp.stack(jnp.split(stacked, lax.axis_size("head"), axis=2)), "head", 0, 0),
+        axis=1,
+    )
     full_keys = arrived_kv[0]
     full_values = arrived_kv[1]
     prompt_keep = jnp.repeat(head_keep, per_prompt, axis=0)

time: 329 us -> 326 us (level)
  waiting for transfers between devices: 246 us -> 234 us
  local copies, waits for them, and re-layouts: 5.61 us -> 14.7 us
    all_to_all x1, waiting for transfers between devices: 13.6 us -> 3.3 us  [per_device(): lax.all_to_all(grouped, 'var', split_axis=0, concat_axis=0, tiled=True)]
    unnamed x8 -> x23, local copies, waits for them, and re-layouts: 1.55 us -> 10.9 us
  transfers between devices with their start and end apart: 5 -> 5, of which waited for: 5 -> 5; matrix products, arithmetic and copies ran while one was open for 6% -> 10% of each run, Pallas kernels for 0% -> 0%
where the time goes in v1:
time: 326 us
  waiting for transfers between devices  234 us (72%)
  starting transfers between devices  35.9 us (11%)
  matrix products  23.6 us (7%)
  local copies, waits for them, and re-layouts  14.7 us (5%)
  between operations  14.2 us (4%)
    reduce_scatter x1, waiting for transfers between devices, project(): lax.psum_scatter(partial_value.astype(jnp.bfloat16), 'head', scatter_dime...  162 us
    all_to_all x1, waiting for transfers between devices, per_device(): lax.all_to_all(jnp.stack(jnp.split(stacked, lax.axis_size('head'), axis=2...  50.3 us
    all_to_all x1, waiting for transfers between devices, per_device(): lax.all_to_all(head_out.reshape(var_count, per_prompt, feature_count), 'v...  15.4 us
    all_to_all x1, starting transfers between devices, per_device(): lax.all_to_all(jnp.stack(jnp.split(stacked, lax.axis_size('head'), axis=2...  14.6 us
    sub x2, matrix products, attend(): exponent = jnp.exp(scores - row_max)  12.2 us
    all_to_all x1, starting transfers between devices, per_device(): lax.all_to_all(head_out.reshape(var_count, per_prompt, feature_count), 'v...  11.7 us
    unnamed x23, local copies, waits for them, and re-layouts  10.9 us
    all_to_all x1, starting transfers between devices, per_device(): lax.all_to_all(grouped, 'var', split_axis=0, concat_axis=0, tiled=True)  9.34 us
  transfers between devices with their start and end apart: 5, of which 5 were waited for; matrix products, arithmetic and copies ran while one was open for 10% of the time, Pallas kernels for 0%

profile of v1, /device:TPU:8, one launch (start us, length us, event | category | flops | bytes accessed | tf_op | source)
XLA Modules:
  0.0 325.7 jit_solution(12128147125843039491)
XLA Ops:
  6.5 9.3 %all-to-all-start.1 = ((bf16[32,16,512]{2,1,0:T(8,128)(2,1)}), bf16[32,16,512]{2,1,0:T(8,128)(2,1)S(1)}, u32[]{:S(2)}, u32[]{:S(2)}) async-start(bf16[32,16,512]{2,1,0:T(8,128)(2,1)} %bitcast.170), calls=%async_computation.1 | async-start | bytes 1048576 | tf_op jit(solution)/shard_map/all_to_all | solution.py:75
  15.9 1.2 copy_bitcast_fusion
  17.0 0.3 broadcast_in_dim.27
  17.3 0.6 fusion.56
  18.0 0.6 fusion.55
  18.6 0.6 fusion.54
  19.2 0.6 fusion.53
  19.9 0.6 fusion.52
  20.5 0.6 fusion.51
  21.1 0.6 fusion.50
  21.7 0.6 fusion.49
  22.4 0.6 fusion.48
  23.0 0.6 fusion.47
  23.6 0.6 fusion.46
  24.2 0.6 fusion.45
  24.8 0.6 fusion.44
  25.5 0.6 fusion.43
  26.1 0.6 fusion.42
  26.7 0.6 fusion.41
  27.4 3.3 %all-to-all-done.1 = bf16[32,16,512]{2,1,0:T(8,128)(2,1)S(1)} async-done(((bf16[32,16,512]{2,1,0:T(8,128)(2,1)}), bf16[32,16,512]{2,1,0:T(8,128)(2,1)S(1)}, u32[]{:S(2)}, u32[]{:S(2)}) %all-to-all-start.1) | async-done | bytes 524320 | tf_op jit(solution)/shard_map/all_to_all | solution.py:75
  30.7 14.6 %all-to-all-start = ((bf16[16,2,128,1,128]{4,2,3,1,0:T(8,128)(2,1)}), bf16[16,2,128,1,128]{4,2,3,1,0:T(8,128)(2,1)S(1)}, u32[]{:S(2)}, u32[]{:S(2)}) async-start(bf16[16,2,128,1,128]{4,2,3,1,0:T(8,128)(2,1)} %fusion.41), calls=%async_computation | async-start | bytes 2097152 | tf_op jit(solution)/shard_map/all_to_all | solution.py:64
  45.3 0.0 all-gather.2.cloned.1.call-start
  45.4 0.7 all-gather.2.cloned.1.call-update
  46.7 0.1 reshape.78
  46.8 0.4 fusion.62
  47.2 50.3 %all-to-all-done = bf16[16,2,128,1,128]{4,2,3,1,0:T(8,128)(2,1)S(1)} async-done(((bf16[16,2,128,1,128]{4,2,3,1,0:T(8,128)(2,1)}), bf16[16,2,128,1,128]{4,2,3,1,0:T(8,128)(2,1)S(1)}, u32[]{:S(2)}, u32[]{:S(2)}) %all-to-all-start) | async-done | bytes 1048608 | tf_op jit(solution)/shard_map/all_to_all | solution.py:64
  97.5 0.1 fusion.61
  97.6 6.1 %fusion.68 = (f32[2,512]{1,0:T(2,128)S(1)}, f32[2,512,2048]{1,2,0:T(8,128)}) fusion(pred[2048]{0:T(1024)(128)(4,1)S(1)} %iota_compare_fusion, bf16[2048,128,1]{1,0,2:T(8,128)(2,1)S(1)} %bitcast.174, bf16[512,2,128]{2,1,0:T(2,128)(2,1)S(1)} %get-tuple-element.7), kind=kOutput, calls=%fused_computation.83 | convolution fusion | flops 545261568 | bytes 9181184 | tf_op jit(solution)/shard_map/sub | solution.py:32
  103.7 6.1 %fusion.63 = (f32[2,512]{1,0:T(2,128)S(1)}, f32[2,512,2048]{1,2,0:T(8,128)}) fusion(pred[2048]{0:T(1024)(128)(4,1)S(1)} %iota_compare_fusion, bf16[2048,128,1]{1,0,2:T(8,128)(2,1)S(1)} %bitcast.175, bf16[512,2,128]{2,1,0:T(2,128)(2,1)S(1)} %get-tuple-element.8), kind=kOutput, calls=%fused_computation.82 | convolution fusion | flops 545261568 | bytes 9181184 | tf_op jit(solution)/shard_map/sub | solution.py:32
  109.8 0.0 copy-start.3
  109.8 4.3 %fusion.20 = bf16[512,2,128]{0,2,1:T(8,128)(2,1)S(1)} fusion(bf16[2048,128,1]{1,0,2:T(8,128)(2,1)S(1)} %bitcast.172, f32[2,512,2048]{1,2,0:T(8,128)} %get-tuple-element.12, f32[2,512]{1,0:T(2,128)S(1)} %get-tuple-element.11), kind=kOutput, calls=%fused_computation.25 | convolution fusion | flops 541196288 | bytes 9179136 | tf_op jit(solution)/shard_map/hrt,td->rhd/dot_general | solution.py:34
  114.1 1.5 copy-done.3
  115.6 0.0 copy-start.1
  115.6 0.0 copy-start.2
  115.6 0.8 fusion.21
  116.4 0.3 copy.72
  116.8 1.0 reshape.79
  117.7 11.7 %all-to-all-start.2 = ((bf16[32,16,512]{2,1,0:T(8,128)(2,1)}), bf16[32,16,512]{2,1,0:T(8,128)(2,1)S(1)}, u32[]{:S(2)}, u32[]{:S(2)}) async-start(bf16[32,16,512]{2,1,0:T(8,128)(2,1)} %reshape.79), calls=%async_computation.2 | async-start | bytes 1048576 | tf_op jit(solution)/shard_map/all_to_all | solution.py:79
  129.4 0.2 reduce-scatter.2.cloned.1.call-start
  129.7 0.0 copy-done.1
  129.7 0.1 broadcast_in_dim.30
  129.7 0.1 reshape.81
  129.9 0.0 copy-done.2
  129.9 0.1 select_convert_fusion
  129.9 0.2 copy.73
  130.1 0.0 copy-start
  130.1 15.4 %all-to-all-done.2 = bf16[32,16,512]{2,1,0:T(8,128)(2,1)S(1)} async-done(((bf16[32,16,512]{2,1,0:T(8,128)(2,1)}), bf16[32,16,512]{2,1,0:T(8,128)(2,1)S(1)}, u32[]{:S(2)}, u32[]{:S(2)}) %all-to-all-start.2) | async-done | bytes 524320 | tf_op jit(solution)/shard_map/all_to_all | solution.py:79
  145.5 2.8 all-gather.2.cloned.1.call-done
  148.3 0.6 mul.25
  149.0 6.5 %convolution_convert_fusion = bf16[512,4096]{1,0:T(8,128)(2,1)} fusion(bf16[512,4096]{1,0:T(8,128)(2,1)} %all-gather.2.cloned.1.call-done, bf16[512,512]{1,0:T(8,128)(2,1)S(1)} %bitcast.171, bf16[64,8,4,128]{3,2,1,0:T(4,128)(2,1)S(1)} %bitcast.169), kind=kOutput, calls=%fused_computation.14 | convolution fusion | flops 2149842944 | bytes 9437184 | tf_op jit(solution)/shard_map/dot_general | solution.py:42
  155.4 0.0 reduce-scatter.2.cloned.1.call-update
  155.5 161.7 %reduce-scatter.2.cloned.1.call-done = bf16[512,256]{1,0:T(8,128)(2,1)} async-done(((bf16[512,4096]{1,0:T(8,128)(2,1)}), bf16[512,256]{1,0:T(8,128)(2,1)}) %reduce-scatter.2.cloned.1.call-update) | async-done | bytes 262160 | tf_op jit(solution)/shard_map/reduce_scatter | solution.py:47
  317.2 0.0 copy-done
  317.2 1.7 add_convert_fusion
  (3 shorter events, 0.1 us)
Async XLA Ops:
  6.5 24.1 %all-to-all-start.1 = ((bf16[32,16,512]{2,1,0:T(8,128)(2,1)}), bf16[32,16,512]{2,1,0:T(8,128)(2,1)S(1)}, u32[]{:S(2)}, u32[]{:S(2)}) async-start(bf16[32,16,512]{2,1,0:T(8,128)(2,1)} %bitcast.170), calls=%async_computation.1 | async-start | bytes 1048576 | tf_op jit(solution)/shard_map/all_to_all | solution.py:75
  30.7 66.9 %all-to-all-start = ((bf16[16,2,128,1,128]{4,2,3,1,0:T(8,128)(2,1)}), bf16[16,2,128,1,128]{4,2,3,1,0:T(8,128)(2,1)S(1)}, u32[]{:S(2)}, u32[]{:S(2)}) async-start(bf16[16,2,128,1,128]{4,2,3,1,0:T(8,128)(2,1)} %fusion.41), calls=%async_computation | async-start | bytes 2097152 | tf_op jit(solution)/shard_map/all_to_all | solution.py:64
  45.3 103.0 %all-gather.2.cloned.1.call-start = ((), (), s32[]{:S(2)}) async-start(), calls=%async_computation.4 | async-start | bytes 4325376 | tf_op jit(solution)/shard_map/all_gather | solution.py:44
  109.8 5.8 %copy-start.3 = (f32[2,512,2048]{1,2,0:T(8,128)S(1)}, f32[2,512,2048]{1,2,0:T(8,128)}, u32[]{:S(2)}) copy-start(f32[2,512,2048]{1,2,0:T(8,128)} %get-tuple-element.10) | copy-start | bytes 25165828
  115.6 14.1 %copy-start.1 = (s32[32,4]{0,1:T(4,128)S(1)}, s32[32,4]{0,1:T(4,128)}, u32[]{:S(2)}) copy-start(s32[32,4]{0,1:T(4,128)} %param.10) | copy-start | bytes 1540
  115.6 14.3 %copy-start.2 = (s32[512]{0:T(512)S(1)}, s32[512]{0:T(512)}, u32[]{:S(2)}) copy-start(s32[512]{0:T(512)} %param.9) | copy-start | bytes 6148
  117.7 27.8 %all-to-all-start.2 = ((bf16[32,16,512]{2,1,0:T(8,128)(2,1)}), bf16[32,16,512]{2,1,0:T(8,128)(2,1)S(1)}, u32[]{:S(2)}, u32[]{:S(2)}) async-start(bf16[32,16,512]{2,1,0:T(8,128)(2,1)} %reshape.79), calls=%async_computation.2 | async-start | bytes 1048576 | tf_op jit(solution)/shard_map/all_to_all | solution.py:79
  129.4 187.8 %reduce-scatter.2.cloned.1.call-start = ((), (), s32[]{:S(2)}) async-start(), calls=%async_computation.5 | async-start | bytes 4456448 | tf_op jit(solution)/shard_map/reduce_scatter | solution.py:47
  130.1 187.1 %copy-start = (bf16[512,256]{1,0:T(8,128)(2,1)S(1)}, bf16[512,256]{1,0:T(8,128)(2,1)}, u32[]{:S(2)}) copy-start(bf16[512,256]{1,0:T(8,128)(2,1)} %param.15) | copy-start | bytes 786436
Sparse Core Ops, SparseCore 0:
  48.2 100.1 all-gather.1
  155.6 161.5 reduce-scatter.1
